TPU v7x, 128 devices: a whole 4x4x4 slice. The times are simulated.
128 devices in a mesh: agent: 8 (over z, core), chan: 8 (over y, x_hi), batch: 2 (over x_lo).
Axes of the slice: x: 4 (x_hi: 2, x_lo: 2; x = x_hi * 2 + x_lo), y: 4, z: 4, core: 2. Of those that a mesh axis runs over, the one named last changes fastest.
Arguments:
- features: bfloat16 [256, 16, 16384], P(None, None, ('agent', 'chan', 'batch')), may hold values from -6 to 6
- norm_gain: float32 [256], replicated, may hold values from 0.1 to 1.9
- tok_in: bfloat16 [16384, 2048], P('agent'), may hold values from -0.046875 to 0.046875
- tok_out: bfloat16 [2048, 16384], P(None, 'agent'), may hold values from -0.125 to 0.125
- mix_gain: float32 [256], replicated, may hold values from 0.1 to 1.9
- chan_in: bfloat16 [256, 1024], replicated, may hold values from -0.375 to 0.375
- chan_out: bfloat16 [1024, 256], replicated, may hold values from -0.1875 to 0.1875
- head: bfloat16 [256, 8], replicated, may hold values from -8 to 8
- actions: int32 [16, 16384], P(None, ('agent', 'chan', 'batch')), may hold values from 0 to 7
- order: int32 [16384], P(('agent', 'chan', 'batch')), may hold values from 0 to 16383, as said below
Outputs:
- input_grad: float32 [256, 16, 16384], P(None, None, ('agent', 'chan', 'batch'))
- head_grad: float32 [256, 8], replicated
Inputs may be any that keep to these rules, and one draw needn't show every extreme that they name: order maps each aligned block of 128 agents one to one onto the same block.
All inputs are finite; a program needn't handle non-finite values.
Results may differ from a plain program's by a relative error of at most 0.025.
Values may be sent and summed in bfloat16 or wider, within the bound.
A program may use at most 128 MiB of HBM per device.

v0:
```python
import jax
import jax.numpy as jnp
from jax import lax
from jax.sharding import PartitionSpec as P

A = 16384
GELU_K = 0.7978845608028654
GELU_C = 0.044715
EPS = 1e-05


def gelu_value(v):
    return 0.5 * v * (1.0 + jnp.tanh(GELU_K * (v + GELU_C * v * v * v)))


def gelu_slope(v):
    inner = jnp.tanh(GELU_K * (v + GELU_C * v * v * v))
    return 0.5 * (1.0 + inner) + 0.5 * v * (1.0 - inner * inner) * GELU_K * (
        1.0 + 3.0 * GELU_C * v * v
    )


def shaped_gain(gain, field):
    return gain.reshape((gain.shape[0],) + (1,) * (field.ndim - 1))


def norm_forward(field, gain):
    center = jnp.mean(field, axis=0, keepdims=True)
    spread = jnp.mean(jnp.square(field - center), axis=0, keepdims=True)
    scale = lax.rsqrt(spread + EPS)
    unit = (field - center) * scale
    return (unit * shaped_gain(gain, field), unit, scale)


def norm_backward(upstream, gain, unit, scale):
    weighted = upstream * shaped_gain(gain, upstream)
    return scale * (
        weighted
        - jnp.mean(weighted, axis=0, keepdims=True)
        - unit * jnp.mean(weighted * unit, axis=0, keepdims=True)
    )


def to_tokens(field):
    return lax.all_to_all(field, ("chan", "batch"), split_axis=0, concat_axis=2, tiled=True)


def to_channels(field):
    return lax.all_to_all(field, ("chan", "batch"), split_axis=2, concat_axis=0, tiled=True)


def project(weight, hidden_dim, rows):
    agent_dim = 1 - hidden_dim
    partial_sum = lax.dot_general(
        weight, rows, (((agent_dim,), (1,)), ((), ())), preferred_element_type=jnp.float32
    )
    return lax.psum(partial_sum, "agent")


def expand(spread, weight, hidden_dim):
    return lax.dot_general(
        spread, weight, (((0,), (hidden_dim,)), ((), ())), preferred_element_type=jnp.float32
    )


def shards(features, norm_gain, tok_in, tok_out, mix_gain, chan_in, chan_out, head, actions, order):
    wide = features.astype(jnp.float32)
    chans, samples, local = wide.shape
    normed_in, unit_in, scale_in = norm_forward(wide, norm_gain)
    spread_in = to_tokens(normed_in.astype(jnp.bfloat16))
    token_chans, _, agents = spread_in.shape
    token_rows = spread_in.reshape(token_chans * samples, agents)
    hidden_pre = project(tok_in, 1, token_rows)
    hidden_act = gelu_value(hidden_pre).astype(jnp.bfloat16)
    mixed = (
        expand(hidden_act, tok_out, 0).astype(jnp.bfloat16).reshape(token_chans, samples, agents)
    )
    mixed_back = to_channels(mixed)
    first = wide + mixed_back.astype(jnp.float32)
    normed_mid, unit_mid, scale_mid = norm_forward(first, mix_gain)
    flat_mid = normed_mid.astype(jnp.bfloat16).reshape(chans, samples * local)
    inner_pre = lax.dot_general(
        chan_in, flat_mid, (((0,), (0,)), ((), ())), preferred_element_type=jnp.float32
    )
    inner = gelu_value(inner_pre).astype(jnp.bfloat16)
    outer = lax.dot_general(
        chan_out, inner, (((0,), (0,)), ((), ())), preferred_element_type=jnp.float32
    )
    second = (first.reshape(chans, samples * local) + outer).astype(jnp.bfloat16)
    logits = lax.dot_general(
        head, second, (((0,), (0,)), ((), ())), preferred_element_type=jnp.float32
    )
    target = jnp.take_along_axis(actions, (order % local)[None, :], axis=1).reshape(
        1, samples * local
    )
    phases = lax.broadcasted_iota(jnp.int32, logits.shape, 0)
    picked = (phases == target).astype(jnp.float32)
    top = jnp.max(logits, axis=0, keepdims=True)
    exps = jnp.exp(logits - top)
    probs = exps / jnp.sum(exps, axis=0, keepdims=True)
    slope = (probs - picked).astype(jnp.bfloat16)
    head_part = lax.dot_general(
        second, slope, (((1,), (1,)), ((), ())), preferred_element_type=jnp.float32
    )
    head_total = lax.psum(head_part, ("agent", "chan", "batch"))
    head_grad = head_total * (1.0 / (samples * A))
    back_second = lax.dot_general(
        head, slope, (((1,), (0,)), ((), ())), preferred_element_type=jnp.float32
    )
    back_low = back_second.astype(jnp.bfloat16)
    back_inner = lax.dot_general(
        chan_out, back_low, (((1,), (0,)), ((), ())), preferred_element_type=jnp.float32
    )
    back_inner_pre = (back_inner * gelu_slope(inner_pre)).astype(jnp.bfloat16)
    back_mid = lax.dot_general(
        chan_in, back_inner_pre, (((1,), (0,)), ((), ())), preferred_element_type=jnp.float32
    )
    back_first = back_second.reshape(chans, samples, local) + norm_backward(
        back_mid.reshape(chans, samples, local), mix_gain, unit_mid, scale_mid
    )
    back_tokens = to_tokens(back_first.astype(jnp.bfloat16))
    back_rows = back_tokens.reshape(token_chans * samples, agents)
    back_hidden = project(tok_out, 0, back_rows)
    back_hidden_pre = (back_hidden * gelu_slope(hidden_pre)).astype(jnp.bfloat16)
    back_spread = (
        expand(back_hidden_pre, tok_in, 1)
        .astype(jnp.bfloat16)
        .reshape(token_chans, samples, agents)
    )
    back_norm = to_channels(back_spread)
    input_grad = back_first + norm_backward(
        back_norm.astype(jnp.float32), norm_gain, unit_in, scale_in
    )
    return (input_grad, head_grad)


def solution(mesh):
    in_specs = (
        P(None, None, ("agent", "chan", "batch")),
        P(),
        P("agent", None),
        P(None, "agent"),
        P(),
        P(),
        P(),
        P(),
        P(None, ("agent", "chan", "batch")),
        P(("agent", "chan", "batch")),
    )
    out_specs = (P(None, None, ("agent", "chan", "batch")), P())
    return jax.shard_map(shards, mesh=mesh, in_specs=in_specs, out_specs=out_specs, check_vma=False)
```

profile of v0, /device:TPU:1, one launch (start us, length us, event | category | flops | bytes accessed | tf_op | source)
XLA Modules:
  0.0 469.4 jit_solution(13224073951282337597)
XLA Ops:
  7.2 1.6 convert_reduce_fusion
  8.9 1.5 fusion.21
  10.4 0.4 fusion.16
  10.8 23.5 %all_to_all.48 = bf16[256,16,128]{2,1,0:T(8,128)(2,1)S(1)} all-to-all(bf16[256,16,128]{2,1,0:T(8,128)(2,1)S(1)} %fusion.16), channel_id=1, replica_groups=mesh['agent'=8,'chan'=8,'batch'=2] {'chan','batch'}, dimensions={0} | all-to-all | bytes 2097152 | tf_op jit(solution)/shard_map/all_to_all | solution.py:45
  34.3 0.7 copy.56
  35.0 7.0 %convolution_bitcast_fusion.1 = f32[2048,256]{0,1:T(8,128)} fusion(bf16[2048,2048]{1,0:T(8,128)(2,1)} %param.12, bf16[32,8,16,128]{3,2,1,0:T(8,128)(2,1)S(1)} %bitcast.134), kind=kOutput, calls=%fused_computation.23 | convolution fusion | flops 2147483648 | bytes 11534336 | tf_op jit(solution)/shard_map/dot_general | solution.py:54
  42.1 64.0 %all-reduce.3.cloned.1.call-done = f32[2048,256]{0,1:T(8,128)} async-done(((f32[2048,256]{0,1:T(8,128)}), f32[2048,256]{0,1:T(8,128)}) %all-reduce.3.cloned.1.call-update) | async-done | bytes 2097168 | tf_op jit(solution)/shard_map/psum | solution.py:57
  106.1 6.6 %convolution_convert_fusion.1 = bf16[256,2048]{1,0:T(8,128)(2,1)S(1)} fusion(bf16[2048,2048]{1,0:T(8,128)(2,1)} %param.13, f32[2048,256]{0,1:T(8,128)} %all-reduce.3.cloned.1.call-done), kind=kOutput, calls=%fused_computation.27 | convolution fusion | flops 2152726528 | bytes 11534336 | tf_op jit(solution)/shard_map/dot_general | solution.py:61
  112.6 8.5 %copy.57 = bf16[16,16,2048]{1,0,2:T(8,128)(2,1)} copy(bf16[16,16,2048]{2,1,0:T(8,128)(2,1)S(1)} %bitcast.133) | data formatting | bytes 2097152 | tf_op jit(solution)/shard_map/reshape | solution.py:76
  121.1 11.2 %reshape.152 = bf16[16,2,16384]{2,1,0:T(2,128)(2,1)} reshape(bf16[2048,16,16]{2,1,0:T(8,128)(2,1)} %bitcast.124) | data formatting | bytes 2097152
  132.4 6.7 %all-to-all-start.1 = ((bf16[16,2,16384]{2,1,0:T(2,128)(2,1)}), bf16[16,2,16384]{2,1,0:T(2,128)(2,1)S(1)}, u32[]{:S(2)}, u32[]{:S(2)}) async-start(bf16[16,2,16384]{2,1,0:T(2,128)(2,1)} %reshape.152), calls=%async_computation.1 | async-start | bytes 2097152 | tf_op jit(solution)/shard_map/all_to_all | solution.py:49
  139.0 0.5 all-reduce.5.cloned.1.call-start
  139.7 0.6 gather_fusion
  140.5 13.1 %all-to-all-done.1 = bf16[16,2,16384]{2,1,0:T(2,128)(2,1)S(1)} async-done(((bf16[16,2,16384]{2,1,0:T(2,128)(2,1)}), bf16[16,2,16384]{2,1,0:T(2,128)(2,1)S(1)}, u32[]{:S(2)}, u32[]{:S(2)}) %all-to-all-start.1) | async-done | bytes 1048608 | tf_op jit(solution)/shard_map/all_to_all | solution.py:49
  153.6 7.5 %reshape.153 = bf16[2048,16,16]{2,1,0:T(8,128)(2,1)} reshape(bf16[16,2,16384]{2,1,0:T(2,128)(2,1)S(1)} %all-to-all-done.1) | data formatting | bytes 2097152
  161.1 10.9 %convert_bitcast_fusion = f32[16,16,16,128]{2,1,3,0:T(8,128)} fusion(bf16[16,16,16,128]{1,0,3,2:T(8,128)(2,1)} %bitcast.123), kind=kLoop, calls=%fused_computation.1 | loop fusion | flops 524288 | bytes 3145728 | tf_op jit(solution)/shard_map/convert_element_type | solution.py:79
  172.0 11.4 %copy.58 = f32[16,16,16,128]{3,2,1,0:T(8,128)} copy(f32[16,16,16,128]{2,1,3,0:T(8,128)} %convert_bitcast_fusion) | data formatting | bytes 4194304 | tf_op jit(solution)/shard_map/convert_element_type | solution.py:79
  183.4 2.2 fusion.76
  185.6 1.8 copy.59
  187.7 0.4 copy-done.13
  188.1 0.4 multiply_convert_fusion.8
  188.5 1.3 fusion.34
  190.1 3.0 fusion.10
  193.2 0.4 fusion.77
  193.6 0.6 copy-done.8
  194.2 1.8 fusion.71
  196.0 9.5 %fusion.29 = (f32[2048]{0:T(1024)S(1)}, f32[2048,256]{1,0:T(8,128)}) fusion(f32[256]{0:T(256)S(1)} %copy-done.13, bf16[256,1024]{1,0:T(8,128)(2,1)S(1)} %copy-done, f32[2048,1024]{1,0:T(8,128)} %copy-done.6, bf16[1024,256]{1,0:T(8,128)(2,1)S(1)} %copy-done.15, f32[2048,256]{1,0:T(8,128)} %fusion.71), kind=kOutput, calls=%fused_computation.48 | convolution fusion | flops 2188376064 | bytes 13640704 | tf_op jit(solution)/shard_map/dot_general | solution.py:115
  205.5 3.1 copy.62
  208.6 3.2 copy.63
  211.8 2.1 multiply_reduce_fusion.1
  214.0 0.6 copy-done.7
  214.7 2.1 fusion.75
  216.7 17.1 %all_to_all.49 = bf16[256,16,128]{2,1,0:T(8,128)(2,1)S(1)} all-to-all(bf16[256,16,128]{2,1,0:T(8,128)(2,1)S(1)} %get-tuple-element.2), channel_id=1, replica_groups=mesh['agent'=8,'chan'=8,'batch'=2] {'chan','batch'}, dimensions={0} | all-to-all | bytes 2097152 | tf_op jit(solution)/shard_map/all_to_all | solution.py:45
  233.8 0.7 copy.64
  234.5 7.0 %convolution_bitcast_fusion = f32[2048,256]{0,1:T(8,128)} fusion(bf16[2048,2048]{1,0:T(8,128)(2,1)} %param.13, bf16[32,8,16,128]{3,2,1,0:T(8,128)(2,1)S(1)} %bitcast.135), kind=kOutput, calls=%fused_computation.22 | convolution fusion | flops 2147483648 | bytes 11534336 | tf_op jit(solution)/shard_map/dot_general | solution.py:54
  241.5 70.8 %all-reduce.5.cloned.1.call-done = f32[2048,256]{0,1:T(8,128)} async-done(((f32[2048,256]{0,1:T(8,128)}), f32[2048,256]{0,1:T(8,128)}) %all-reduce.5.cloned.1.call-update) | async-done | bytes 2097168 | tf_op jit(solution)/shard_map/psum | solution.py:57
  312.3 7.8 %convolution_convert_fusion = bf16[256,2048]{1,0:T(8,128)(2,1)S(1)} fusion(bf16[2048,2048]{1,0:T(8,128)(2,1)} %param.12, f32[2048,256]{0,1:T(8,128)} %all-reduce.5.cloned.1.call-done, f32[2048,256]{0,1:T(8,128)} %all-reduce.3.cloned.1.call-done), kind=kOutput, calls=%fused_computation.26 | convolution fusion | flops 2157969408 | bytes 13631488 | tf_op jit(solution)/shard_map/dot_general | solution.py:61
  320.1 8.5 %copy.65 = bf16[16,16,2048]{1,0,2:T(8,128)(2,1)} copy(bf16[16,16,2048]{2,1,0:T(8,128)(2,1)S(1)} %bitcast.132) | data formatting | bytes 2097152 | tf_op jit(solution)/shard_map/reshape | solution.py:128
  328.6 11.2 %reshape.154 = bf16[16,2,16384]{2,1,0:T(2,128)(2,1)} reshape(bf16[2048,16,16]{2,1,0:T(8,128)(2,1)} %bitcast.125) | data formatting | bytes 2097152
  339.9 6.7 %all-to-all-start.3 = ((bf16[16,2,16384]{2,1,0:T(2,128)(2,1)}), bf16[16,2,16384]{2,1,0:T(2,128)(2,1)S(1)}, u32[]{:S(2)}, u32[]{:S(2)}) async-start(bf16[16,2,16384]{2,1,0:T(2,128)(2,1)} %reshape.154), calls=%async_computation.3 | async-start | bytes 2097152 | tf_op jit(solution)/shard_map/all_to_all | solution.py:49
  346.9 73.3 %psum.23 = f32[256,8]{0,1:T(8,128)S(1)} all-reduce(f32[256,8]{0,1:T(8,128)S(1)} %fusion.69), channel_id=1, replica_groups=mesh['agent'=8,'chan'=8,'batch'=2] {'agent','chan','batch'}, use_global_device_ids=true, to_apply=%region_12.13 | all-reduce | flops 2048 | bytes 16384 | tf_op jit(solution)/shard_map/psum | solution.py:105
  420.2 0.6 broadcast_multiply_fusion
  420.8 7.5 %reshape.155 = bf16[2048,16,16]{2,1,0:T(8,128)(2,1)} reshape(bf16[16,2,16384]{2,1,0:T(2,128)(2,1)S(1)} %all-to-all-done.3) | data formatting | bytes 2097152
  428.3 10.9 %convert_bitcast_fusion.1 = f32[16,16,16,128]{2,1,3,0:T(8,128)} fusion(bf16[2048,16,16]{2,1,0:T(8,128)(2,1)} %reshape.155), kind=kLoop, calls=%fused_computation.2 | loop fusion | flops 524288 | bytes 3145728 | tf_op jit(solution)/shard_map/convert_element_type | solution.py:132
  439.2 5.7 %multiply_reduce_fusion = f32[16,128]{0,1:T(8,128)S(1)} fusion(f32[16,16]{1,0:T(8,128)S(1)} %mul.242, bf16[16,16,16,128]{1,0,3,2:T(8,128)(2,1)} %bitcast.122), kind=kLoop, calls=%fused_computation.3 | loop fusion | flops 1570816 | bytes 1057792 | tf_op jit(solution)/shard_map/reduce_sum | solution.py:39
  445.0 11.5 %copy.66 = f32[16,16,16,128]{3,2,1,0:T(8,128)} copy(f32[16,16,16,128]{2,1,3,0:T(8,128)} %convert_bitcast_fusion.1) | data formatting | bytes 4194304 | tf_op jit(solution)/shard_map/convert_element_type | solution.py:132
  456.5 2.2 fusion.17
  458.7 3.6 fusion.20
  (52 shorter events, 1.5 us)
Async XLA Ops:
  7.2 181.3 %copy-start = (bf16[256,1024]{1,0:T(8,128)(2,1)S(1)}, bf16[256,1024]{1,0:T(8,128)(2,1)}, u32[]{:S(2)}) copy-start(bf16[256,1024]{1,0:T(8,128)(2,1)} %param.15) | copy-start | bytes 1572868
  7.2 3.2 copy-start.2
  7.2 3.2 copy-start.12
  7.2 98.9 %all-reduce.3.cloned.1.call-start = ((), (), s32[]{:S(2)}) async-start(), calls=%async_computation.4 | async-start | bytes 4194304 | tf_op jit(solution)/shard_map/psum | solution.py:57
  132.4 7.2 %copy-start.14 = (s32[16,128]{1,0:T(8,128)S(1)}, s32[16,128]{1,0:T(8,128)}, u32[]{:S(2)}) copy-start(s32[16,128]{1,0:T(8,128)} %param.18) | copy-start | bytes 24580
  132.4 7.3 %copy-start.16 = (s32[128]{0:T(128)S(1)}, s32[128]{0:T(128)}, u32[]{:S(2)}) copy-start(s32[128]{0:T(128)} %param.19) | copy-start | bytes 1540
  132.4 21.2 %all-to-all-start.1 = ((bf16[16,2,16384]{2,1,0:T(2,128)(2,1)}), bf16[16,2,16384]{2,1,0:T(2,128)(2,1)S(1)}, u32[]{:S(2)}, u32[]{:S(2)}) async-start(bf16[16,2,16384]{2,1,0:T(2,128)(2,1)} %reshape.152), calls=%async_computation.1 | async-start | bytes 2097152 | tf_op jit(solution)/shard_map/all_to_all | solution.py:49
  139.0 173.2 %all-reduce.5.cloned.1.call-start = ((), (), s32[]{:S(2)}) async-start(), calls=%async_computation.5 | async-start | bytes 4194304 | tf_op jit(solution)/shard_map/psum | solution.py:57
  187.4 0.7 copy-start.13
  188.4 1.6 copy-start.10
  188.5 1.7 copy-start.15
  189.8 3.3 copy-start.6
  190.1 3.0 copy-start.11
  193.2 1.0 copy-start.8
  211.8 2.2 copy-start.4
  211.8 2.8 copy-start.7
  339.9 6.7 %copy-start.9 = (bf16[256,2048]{0,1:T(8,128)(2,1)S(1)}, bf16[256,2048]{0,1:T(8,128)(2,1)}, u32[]{:S(2)}) copy-start(bf16[256,2048]{0,1:T(8,128)(2,1)} %copy-done.8) | copy-start | bytes 3145732
  339.9 80.9 %all-to-all-start.3 = ((bf16[16,2,16384]{2,1,0:T(2,128)(2,1)}), bf16[16,2,16384]{2,1,0:T(2,128)(2,1)S(1)}, u32[]{:S(2)}, u32[]{:S(2)}) async-start(bf16[16,2,16384]{2,1,0:T(2,128)(2,1)} %reshape.154), calls=%async_computation.3 | async-start | bytes 2097152 | tf_op jit(solution)/shard_map/all_to_all | solution.py:49
  444.9 11.5 %copy-start.3 = (bf16[256,16,128]{2,1,0:T(8,128)(2,1)S(1)}, bf16[256,16,128]{2,1,0:T(8,128)(2,1)}, u32[]{:S(2)}) copy-start(bf16[256,16,128]{2,1,0:T(8,128)(2,1)} %param.10) | copy-start | bytes 3145732
  456.5 2.2 copy-start.5
  458.7 3.6 copy-start.1
Sparse Core Ops, SparseCore 0:
  42.2 63.8 all-reduce.2
  241.7 70.5 all-reduce.4
where the time goes:
time: 477 us; the launch traced here: 469 us
  waiting for transfers between devices  148 us (31%)
  blocking collectives  114 us (24%)
  local copies, waits for them, and re-layouts  89.9 us (19%)
  matrix products  44.8 us (9%)
  other arithmetic  44.6 us (9%)
  between operations  14.6 us (3%)
  starting transfers between devices  13.9 us (3%)
    psum x2, waiting for transfers between devices, project(): return lax.psum(partial_sum, 'agent')  135 us
    psum x1, blocking collectives, shards(): head_total = lax.psum(head_part, ('agent', 'chan', 'batch'))  73.3 us
    all_to_all x2, blocking collectives, to_tokens(): lax.all_to_all(field, ('chan', 'batch'), split_axis=0, concat_axis=2, til...  40.6 us
    unnamed x39, local copies, waits for them, and re-layouts  39.6 us
    dot_general x2, matrix products, expand(): lax.dot_general(spread, weight, (((0,), (hidden_dim,)), ((), ())), prefer...  14.4 us
    dot_general x2, matrix products, project(): lax.dot_general(weight, rows, (((agent_dim,), (1,)), ((), ())), preferred...  14.1 us
    all_to_all x2, starting transfers between devices, to_channels(): lax.all_to_all(field, ('chan', 'batch'), split_axis=2, concat_axis=0, til...  13.3 us
    all_to_all x2, waiting for transfers between devices, to_channels(): lax.all_to_all(field, ('chan', 'batch'), split_axis=2, concat_axis=0, til...  13.1 us
  transfers between devices with their start and end apart: 4, of which 3 were waited for; matrix products, arithmetic and copies ran while one was open for 0% of the time, Pallas kernels for 0%

commit v1 on v0

--- a/solution.py
+++ b/solution.py
@@ -102,7 +102,9 @@
     head_part = lax.dot_general(
         second, slope, (((1,), (1,)), ((), ())), preferred_element_type=jnp.float32
     )
-    head_total = lax.psum(head_part, ("agent", "chan", "batch"))
+    head_total = head_part
+    for j0 in (("chan", "batch"), "agent"):
+        head_total = jax.lax.psum(head_total, axis_name=j0)
     head_grad = head_total * (1.0 / (samples * A))
     back_second = lax.dot_general(
         head, slope, (((1,), (0,)), ((), ())), preferred_element_type=jnp.float32

time: 477 us -> 459 us (0.962); the launches traced: 469 us -> 457 us
  blocking collectives: 114 us -> 102 us
    psum x1 -> x2, blocking collectives: 73.3 us -> 61.4 us  [shards(): head_total = jax.lax.psum(head_total, axis_name=j0)]
where the time goes in v1:
time: 459 us; the launch traced here: 457 us
  waiting for transfers between devices  148 us (32%)
  blocking collectives  102 us (22%)
  local copies, waits for them, and re-layouts  89.7 us (20%)
  matrix products  44.8 us (10%)
  other arithmetic  44.6 us (10%)
  between operations  14.3 us (3%)
  starting transfers between devices  13.6 us (3%)
    psum x2, waiting for transfers between devices, project(): return lax.psum(partial_sum, 'agent')  135 us
    psum x2, blocking collectives, shards(): head_total = jax.lax.psum(head_total, axis_name=j0)  61.4 us
    all_to_all x2, blocking collectives, to_tokens(): lax.all_to_all(field, ('chan', 'batch'), split_axis=0, concat_axis=2, til...  40.6 us
    unnamed x39, local copies, waits for them, and re-layouts  39.7 us
    dot_general x2, matrix products, expand(): lax.dot_general(spread, weight, (((0,), (hidden_dim,)), ((), ())), prefer...  14.4 us
    dot_general x2, matrix products, project(): lax.dot_general(weight, rows, (((agent_dim,), (1,)), ((), ())), preferred...  14.1 us
    all_to_all x2, waiting for transfers between devices, to_channels(): lax.all_to_all(field, ('chan', 'batch'), split_axis=2, concat_axis=0, til...  13.4 us
    all_to_all x2, starting transfers between devices, to_channels(): lax.all_to_all(field, ('chan', 'batch'), split_axis=2, concat_axis=0, til...  13.3 us
  transfers between devices with their start and end apart: 4, of which 3 were waited for; matrix products, arithmetic and copies ran while one was open for 0% of the time, Pallas kernels for 0%

profile of v1, /device:TPU:1, one launch (start us, length us, event | category | flops | bytes accessed | tf_op | source)
XLA Modules:
  0.0 457.1 jit_solution(11943538280089385710)
XLA Ops:
  7.2 1.6 convert_reduce_fusion
  8.9 1.5 fusion.21
  10.4 0.4 fusion.16
  10.8 23.5 %all_to_all.48 = bf16[256,16,128]{2,1,0:T(8,128)(2,1)S(1)} all-to-all(bf16[256,16,128]{2,1,0:T(8,128)(2,1)S(1)} %fusion.16), channel_id=1, replica_groups=mesh['agent'=8,'chan'=8,'batch'=2] {'chan','batch'}, dimensions={0} | all-to-all | bytes 2097152 | tf_op jit(solution)/shard_map/all_to_all | solution.py:45
  34.3 0.7 copy.56
  35.0 7.0 %convolution_bitcast_fusion.1 = f32[2048,256]{0,1:T(8,128)} fusion(bf16[2048,2048]{1,0:T(8,128)(2,1)} %param.12, bf16[32,8,16,128]{3,2,1,0:T(8,128)(2,1)S(1)} %bitcast.134), kind=kOutput, calls=%fused_computation.23 | convolution fusion | flops 2147483648 | bytes 11534336 | tf_op jit(solution)/shard_map/dot_general | solution.py:54
  42.1 64.0 %all-reduce.3.cloned.1.call-done = f32[2048,256]{0,1:T(8,128)} async-done(((f32[2048,256]{0,1:T(8,128)}), f32[2048,256]{0,1:T(8,128)}) %all-reduce.3.cloned.1.call-update) | async-done | bytes 2097168 | tf_op jit(solution)/shard_map/psum | solution.py:57
  106.1 6.6 %convolution_convert_fusion.1 = bf16[256,2048]{1,0:T(8,128)(2,1)S(1)} fusion(bf16[2048,2048]{1,0:T(8,128)(2,1)} %param.13, f32[2048,256]{0,1:T(8,128)} %all-reduce.3.cloned.1.call-done), kind=kOutput, calls=%fused_computation.27 | convolution fusion | flops 2152726528 | bytes 11534336 | tf_op jit(solution)/shard_map/dot_general | solution.py:61
  112.6 8.5 %copy.57 = bf16[16,16,2048]{1,0,2:T(8,128)(2,1)} copy(bf16[16,16,2048]{2,1,0:T(8,128)(2,1)S(1)} %bitcast.133) | data formatting | bytes 2097152 | tf_op jit(solution)/shard_map/reshape | solution.py:76
  121.1 11.2 %reshape.152 = bf16[16,2,16384]{2,1,0:T(2,128)(2,1)} reshape(bf16[2048,16,16]{2,1,0:T(8,128)(2,1)} %bitcast.124) | data formatting | bytes 2097152
  132.4 6.7 %all-to-all-start.1 = ((bf16[16,2,16384]{2,1,0:T(2,128)(2,1)}), bf16[16,2,16384]{2,1,0:T(2,128)(2,1)S(1)}, u32[]{:S(2)}, u32[]{:S(2)}) async-start(bf16[16,2,16384]{2,1,0:T(2,128)(2,1)} %reshape.152), calls=%async_computation.1 | async-start | bytes 2097152 | tf_op jit(solution)/shard_map/all_to_all | solution.py:49
  139.4 0.6 gather_fusion
  140.2 13.4 %all-to-all-done.1 = bf16[16,2,16384]{2,1,0:T(2,128)(2,1)S(1)} async-done(((bf16[16,2,16384]{2,1,0:T(2,128)(2,1)}), bf16[16,2,16384]{2,1,0:T(2,128)(2,1)S(1)}, u32[]{:S(2)}, u32[]{:S(2)}) %all-to-all-start.1) | async-done | bytes 1048608 | tf_op jit(solution)/shard_map/all_to_all | solution.py:49
  153.6 7.5 %reshape.153 = bf16[2048,16,16]{2,1,0:T(8,128)(2,1)} reshape(bf16[16,2,16384]{2,1,0:T(2,128)(2,1)S(1)} %all-to-all-done.1) | data formatting | bytes 2097152
  161.1 10.9 %convert_bitcast_fusion = f32[16,16,16,128]{2,1,3,0:T(8,128)} fusion(bf16[16,16,16,128]{1,0,3,2:T(8,128)(2,1)} %bitcast.123), kind=kLoop, calls=%fused_computation.1 | loop fusion | flops 524288 | bytes 3145728 | tf_op jit(solution)/shard_map/convert_element_type | solution.py:79
  172.0 11.4 %copy.58 = f32[16,16,16,128]{3,2,1,0:T(8,128)} copy(f32[16,16,16,128]{2,1,3,0:T(8,128)} %convert_bitcast_fusion) | data formatting | bytes 4194304 | tf_op jit(solution)/shard_map/convert_element_type | solution.py:79
  183.4 2.2 fusion.76
  185.6 1.8 copy.59
  187.7 0.4 copy-done.13
  188.1 0.4 multiply_convert_fusion.8
  188.5 1.3 fusion.34
  190.1 3.0 fusion.10
  193.2 0.4 fusion.77
  193.6 0.6 copy-done.8
  194.2 1.8 fusion.71
  196.0 9.5 %fusion.29 = (f32[2048]{0:T(1024)S(1)}, f32[2048,256]{1,0:T(8,128)}) fusion(f32[256]{0:T(256)S(1)} %copy-done.13, bf16[256,1024]{1,0:T(8,128)(2,1)S(1)} %copy-done, f32[2048,1024]{1,0:T(8,128)} %copy-done.6, bf16[1024,256]{1,0:T(8,128)(2,1)S(1)} %copy-done.15, f32[2048,256]{1,0:T(8,128)} %fusion.71), kind=kOutput, calls=%fused_computation.48 | convolution fusion | flops 2188376064 | bytes 13640704 | tf_op jit(solution)/shard_map/dot_general | solution.py:117
  205.5 3.1 copy.62
  208.6 3.0 copy.63
  211.7 2.1 multiply_reduce_fusion.1
  213.9 0.6 copy-done.7
  214.5 2.1 fusion.75
  216.6 17.1 %all_to_all.49 = bf16[256,16,128]{2,1,0:T(8,128)(2,1)S(1)} all-to-all(bf16[256,16,128]{2,1,0:T(8,128)(2,1)S(1)} %get-tuple-element.2), channel_id=1, replica_groups=mesh['agent'=8,'chan'=8,'batch'=2] {'chan','batch'}, dimensions={0} | all-to-all | bytes 2097152 | tf_op jit(solution)/shard_map/all_to_all | solution.py:45
  233.7 0.7 copy.64
  234.3 7.0 %convolution_bitcast_fusion = f32[2048,256]{0,1:T(8,128)} fusion(bf16[2048,2048]{1,0:T(8,128)(2,1)} %param.13, bf16[32,8,16,128]{3,2,1,0:T(8,128)(2,1)S(1)} %bitcast.135), kind=kOutput, calls=%fused_computation.22 | convolution fusion | flops 2147483648 | bytes 11534336 | tf_op jit(solution)/shard_map/dot_general | solution.py:54
  241.4 70.7 %all-reduce.5.cloned.1.call-done = f32[2048,256]{0,1:T(8,128)} async-done(((f32[2048,256]{0,1:T(8,128)}), f32[2048,256]{0,1:T(8,128)}) %all-reduce.5.cloned.1.call-update) | async-done | bytes 2097168 | tf_op jit(solution)/shard_map/psum | solution.py:57
  312.1 7.8 %convolution_convert_fusion = bf16[256,2048]{1,0:T(8,128)(2,1)S(1)} fusion(bf16[2048,2048]{1,0:T(8,128)(2,1)} %param.12, f32[2048,256]{0,1:T(8,128)} %all-reduce.5.cloned.1.call-done, f32[2048,256]{0,1:T(8,128)} %all-reduce.3.cloned.1.call-done), kind=kOutput, calls=%fused_computation.26 | convolution fusion | flops 2157969408 | bytes 13631488 | tf_op jit(solution)/shard_map/dot_general | solution.py:61
  319.9 8.5 %copy.65 = bf16[16,16,2048]{1,0,2:T(8,128)(2,1)} copy(bf16[16,16,2048]{2,1,0:T(8,128)(2,1)S(1)} %bitcast.132) | data formatting | bytes 2097152 | tf_op jit(solution)/shard_map/reshape | solution.py:130
  328.4 11.2 %reshape.154 = bf16[16,2,16384]{2,1,0:T(2,128)(2,1)} reshape(bf16[2048,16,16]{2,1,0:T(8,128)(2,1)} %bitcast.125) | data formatting | bytes 2097152
  339.7 6.7 %all-to-all-start.3 = ((bf16[16,2,16384]{2,1,0:T(2,128)(2,1)}), bf16[16,2,16384]{2,1,0:T(2,128)(2,1)S(1)}, u32[]{:S(2)}, u32[]{:S(2)}) async-start(bf16[16,2,16384]{2,1,0:T(2,128)(2,1)} %reshape.154), calls=%async_computation.3 | async-start | bytes 2097152 | tf_op jit(solution)/shard_map/all_to_all | solution.py:49
  346.7 37.8 %psum.30 = f32[256,8]{0,1:T(8,128)S(1)} all-reduce(f32[256,8]{0,1:T(8,128)S(1)} %fusion.69), channel_id=1, replica_groups=mesh['agent'=8,'chan'=8,'batch'=2] {'chan','batch'}, use_global_device_ids=true, to_apply=%region_12.13 | all-reduce | flops 2048 | bytes 16384 | tf_op jit(solution)/shard_map/psum | solution.py:107
  384.4 23.6 %psum.31 = f32[256,8]{0,1:T(8,128)S(1)} all-reduce(f32[256,8]{0,1:T(8,128)S(1)} %psum.30), channel_id=1, replica_groups=mesh['agent'=8,'chan'=8,'batch'=2] {'agent'}, use_global_device_ids=true, to_apply=%region_13.14 | all-reduce | flops 2048 | bytes 16384 | tf_op jit(solution)/shard_map/psum | solution.py:107
  408.1 0.6 broadcast_multiply_fusion
  408.7 7.5 %reshape.155 = bf16[2048,16,16]{2,1,0:T(8,128)(2,1)} reshape(bf16[16,2,16384]{2,1,0:T(2,128)(2,1)S(1)} %all-to-all-done.3) | data formatting | bytes 2097152
  416.2 10.9 %convert_bitcast_fusion.1 = f32[16,16,16,128]{2,1,3,0:T(8,128)} fusion(bf16[2048,16,16]{2,1,0:T(8,128)(2,1)} %reshape.155), kind=kLoop, calls=%fused_computation.2 | loop fusion | flops 524288 | bytes 3145728 | tf_op jit(solution)/shard_map/convert_element_type | solution.py:134
  427.1 5.7 %multiply_reduce_fusion = f32[16,128]{0,1:T(8,128)S(1)} fusion(f32[16,16]{1,0:T(8,128)S(1)} %mul.242, bf16[16,16,16,128]{1,0,3,2:T(8,128)(2,1)} %bitcast.122), kind=kLoop, calls=%fused_computation.3 | loop fusion | flops 1570816 | bytes 1057792 | tf_op jit(solution)/shard_map/reduce_sum | solution.py:39
  432.9 11.5 %copy.66 = f32[16,16,16,128]{3,2,1,0:T(8,128)} copy(f32[16,16,16,128]{2,1,3,0:T(8,128)} %convert_bitcast_fusion.1) | data formatting | bytes 4194304 | tf_op jit(solution)/shard_map/convert_element_type | solution.py:134
  444.4 2.2 fusion.17
  446.6 3.6 fusion.20
  (53 shorter events, 1.7 us)
Async XLA Ops:
  7.2 181.3 %copy-start = (bf16[256,1024]{1,0:T(8,128)(2,1)S(1)}, bf16[256,1024]{1,0:T(8,128)(2,1)}, u32[]{:S(2)}) copy-start(bf16[256,1024]{1,0:T(8,128)(2,1)} %param.15) | copy-start | bytes 1572868
  7.2 3.2 copy-start.2
  7.2 3.2 copy-start.12
  7.2 98.9 %all-reduce.3.cloned.1.call-start = ((), (), s32[]{:S(2)}) async-start(), calls=%async_computation.4 | async-start | bytes 4194304 | tf_op jit(solution)/shard_map/psum | solution.py:57
  132.4 6.9 %copy-start.14 = (s32[16,128]{1,0:T(8,128)S(1)}, s32[16,128]{1,0:T(8,128)}, u32[]{:S(2)}) copy-start(s32[16,128]{1,0:T(8,128)} %param.18) | copy-start | bytes 24580
  132.4 7.0 %copy-start.16 = (s32[128]{0:T(128)S(1)}, s32[128]{0:T(128)}, u32[]{:S(2)}) copy-start(s32[128]{0:T(128)} %param.19) | copy-start | bytes 1540
  132.4 21.2 %all-to-all-start.1 = ((bf16[16,2,16384]{2,1,0:T(2,128)(2,1)}), bf16[16,2,16384]{2,1,0:T(2,128)(2,1)S(1)}, u32[]{:S(2)}, u32[]{:S(2)}) async-start(bf16[16,2,16384]{2,1,0:T(2,128)(2,1)} %reshape.152), calls=%async_computation.1 | async-start | bytes 2097152 | tf_op jit(solution)/shard_map/all_to_all | solution.py:49
  139.0 173.0 %all-reduce.5.cloned.1.call-start = ((), (), s32[]{:S(2)}) async-start(), calls=%async_computation.5 | async-start | bytes 4194304 | tf_op jit(solution)/shard_map/psum | solution.py:57
  187.4 0.7 copy-start.13
  188.5 1.6 copy-start.10
  188.5 1.7 copy-start.15
  189.8 3.3 copy-start.6
  190.1 3.0 copy-start.11
  193.2 1.0 copy-start.8
  211.7 2.2 copy-start.4
  211.7 2.9 copy-start.7
  339.7 6.8 %copy-start.9 = (bf16[256,2048]{0,1:T(8,128)(2,1)S(1)}, bf16[256,2048]{0,1:T(8,128)(2,1)}, u32[]{:S(2)}) copy-start(bf16[256,2048]{0,1:T(8,128)(2,1)} %copy-done.8) | copy-start | bytes 3145732
  339.7 69.0 %all-to-all-start.3 = ((bf16[16,2,16384]{2,1,0:T(2,128)(2,1)}), bf16[16,2,16384]{2,1,0:T(2,128)(2,1)S(1)}, u32[]{:S(2)}, u32[]{:S(2)}) async-start(bf16[16,2,16384]{2,1,0:T(2,128)(2,1)} %reshape.154), calls=%async_computation.3 | async-start | bytes 2097152 | tf_op jit(solution)/shard_map/all_to_all | solution.py:49
  432.9 11.5 %copy-start.3 = (bf16[256,16,128]{2,1,0:T(8,128)(2,1)S(1)}, bf16[256,16,128]{2,1,0:T(8,128)(2,1)}, u32[]{:S(2)}) copy-start(bf16[256,16,128]{2,1,0:T(8,128)(2,1)} %param.10) | copy-start | bytes 3145732
  444.4 2.2 copy-start.5
  446.6 3.6 copy-start.1
Sparse Core Ops, SparseCore 0:
  42.2 63.8 all-reduce.2
  241.5 70.5 all-reduce.4
